TPU v7x, 256 devices: a whole 4x4x8 slice. The times are simulated.
256 devices in a mesh: node: 64 (over z, x, core), feat: 4 (over y).
Axes of the slice: x: 4, y: 4, z: 8, core: 2. Of those that a mesh axis runs over, the one named last changes fastest.
Arguments:
- features: float32 [49152, 1024], P('node', 'feat'), may hold values from -6 to 6
- degrees: int32 [49152], P('node'), may hold values from 1 to 4
- tile_row: int32 [64, 201], P('node'), may hold values from 0 to 5, as said below
- tile_col: int32 [64, 201], P('node'), may hold values from 0 to 69, as said below
- tile_count: int32 [64], P('node'), may hold values from 75 to 201, as said below
- send_block: int32 [64, 64], replicated, may hold values from 0 to 5
- tile_val: bfloat16 [64, 201, 128, 128], P('node'), may hold values from -0.15625 to 0.15625
- weight: bfloat16 [1024, 3, 1024], P('node', None, 'feat'), may hold values from -0.109375 to 0.109375
- out_bias: float32 [1024], replicated, may hold values from -3 to 3
- cotangent: bfloat16 [49152, 1024], P(('node', 'feat')), may hold values from -0.109375 to 0.109375
Outputs:
- output: bfloat16 [49152, 1024], P(('node', 'feat'))
- weight_grad: float32 [1024, 3, 1024], P('node', None, 'feat')
- bias_grad: float32 [1024], replicated
Inputs may be any that keep to these rules, and one draw needn't show every extreme that they name: `tile_row`: the row block of each slot; for each other part q, between 1 and 3 live tiles of part p read slot 6 + q, each at a different row block. `tile_col`: below 6: the part's own row block; 6 + q: the block that part q sends; the first 12 slots of each part read own blocks, tile i < 6 at row block i, column i; slots past tile_count read 0; no tile reads slot 6 + p in part p. `tile_count`: live tiles come first in each part; some part has 201 live tiles.
All inputs are finite; a program needn't handle non-finite values.
Results may differ from a plain program's by a relative error of at most 0.0057.
Values may be sent and summed in bfloat16 or wider, within the bound.
No kernel may reach another device: no remote copies, remote signals or barrier semaphores. Data moves between devices by JAX's collectives and lax.ppermute only.
A program may use at most 192 MiB of HBM per device.

v0:
```python
import jax
import jax.numpy as jnp
from jax import lax
from jax.sharding import Mesh
from jax.sharding import PartitionSpec as P

HOPS = 2
NODE = ("node_0", "node_1", "node_2")
NODE_FEAT = ("node_0", "node_1", "node_2", "feat")


def sent_to_all(shard, axis):
    devices = lax.axis_size(axis)
    return lax.all_to_all(
        jnp.broadcast_to(shard[None], (devices, *shard.shape)), axis, 0, 0, tiled=True
    )


def laid_out(blocks, dim):
    dims = list(blocks.shape[1:])
    dims[dim] *= blocks.shape[0]
    return jnp.moveaxis(blocks, 0, dim).reshape(dims)


def collect(shard, axis, dim):
    blocks = sent_to_all(shard, axis)
    return laid_out(blocks, dim)


def split_up(shard, dim, devices):
    dims = shard.shape
    blocks = shard.reshape(*dims[:dim], devices, dims[dim] // devices, *dims[dim + 1 :])
    return jnp.moveaxis(blocks, dim, 0)


def sum_at_owner(shard, axis, dim):
    devices = lax.axis_size(axis)
    blocks = lax.all_to_all(split_up(shard, dim, devices), axis, 0, 0, tiled=True)
    return jnp.sum(blocks, axis=0)


def over_axes(shard, axes):
    for axis in axes:
        shard = lax.psum(shard, axis)
    return shard


def propagate(source, tile_rows, tile_cols, tile_values, is_live, send_row):
    block_size = tile_values.shape[-1]
    panel_width = source.shape[1]
    own_blocks = source.reshape(-1, block_size, panel_width)
    outgoing = own_blocks[send_row]
    arrived = lax.all_to_all(outgoing, NODE, split_axis=0, concat_axis=0, tiled=True)
    frame = jnp.concatenate([own_blocks, arrived], axis=0)
    sources = frame[tile_cols]
    product = jnp.einsum("tij,tjc->tic", tile_values, sources, preferred_element_type=jnp.float32)
    block_ids = jnp.arange(own_blocks.shape[0], dtype=jnp.int32)
    onehot = ((tile_rows[:, None] == block_ids[None, :]) & is_live[:, None]).astype(jnp.float32)
    summed = jnp.einsum("tr,tic->ric", onehot, product, precision=lax.Precision.HIGHEST)
    return summed.reshape(source.shape[0], panel_width)


def local(
    features,
    degrees,
    tile_row,
    tile_col,
    tile_count,
    send_block,
    tile_val,
    weight,
    out_bias,
    cotangent,
):
    node_index = lax.axis_index(NODE)
    send_row = lax.dynamic_index_in_dim(send_block, node_index, 0, keepdims=False)
    tile_rows = tile_row[0]
    tile_cols = tile_col[0]
    tile_values = tile_val[0]
    is_live = jnp.arange(tile_rows.shape[0], dtype=jnp.int32) < tile_count[0]
    row_scale = lax.rsqrt(degrees.astype(jnp.float32))[:, None]
    source = (features * row_scale).astype(jnp.bfloat16)
    hop_list = [features.astype(jnp.bfloat16)]
    for hop_number in range(HOPS):
        summed = propagate(source, tile_rows, tile_cols, tile_values, is_live, send_row)
        hop_list.append((summed * row_scale).astype(jnp.bfloat16))
        if hop_number + 1 < HOPS:
            source = (summed * row_scale * row_scale).astype(jnp.bfloat16)
    stacked = jnp.stack(hop_list, axis=1)
    hop_total = stacked.shape[1]
    flat_rows = stacked.reshape(stacked.shape[0], -1)
    piece = collect(weight, NODE, 0)
    flat_piece = piece.reshape(piece.shape[0], -1)
    panel_terms = lax.dot_general(
        flat_rows, flat_piece, (((1,), (1,)), ((), ())), preferred_element_type=jnp.float32
    )
    linear = sum_at_owner(panel_terms, "feat", 0)
    linear = linear + out_bias[None, :]
    sigmoid_val = jax.nn.sigmoid(linear)
    output = (linear * sigmoid_val).astype(jnp.bfloat16)
    grad_linear = (
        cotangent.astype(jnp.float32) * sigmoid_val * (1.0 + linear * (1.0 - sigmoid_val))
    ).astype(jnp.bfloat16)
    bias_grad = over_axes(jnp.sum(grad_linear.astype(jnp.float32), axis=0), NODE_FEAT)
    grad_all = collect(grad_linear, "feat", 0)
    term = lax.dot_general(
        grad_all, flat_rows, (((0,), (0,)), ((), ())), preferred_element_type=jnp.float32
    )
    weight_grad = sum_at_owner(
        term.reshape(weight.shape[0] * lax.axis_size(NODE), hop_total, -1), NODE, 0
    )
    return (output, weight_grad, bias_grad)


def solution(mesh):
    split = Mesh(
        mesh.devices.reshape(8, 4, 2, mesh.shape["feat"]), ("node_0", "node_1", "node_2", "feat")
    )
    return jax.shard_map(
        local,
        mesh=split,
        in_specs=(
            P(NODE, "feat"),
            P(NODE),
            P(NODE, None),
            P(NODE, None),
            P(NODE),
            P(),
            P(NODE, None, None, None),
            P(NODE, None, "feat"),
            P(),
            P(NODE_FEAT, None),
        ),
        out_specs=(P(NODE_FEAT, None), P(NODE, None, "feat"), P()),
        check_vma=False,
    )
```

profile of v0, /device:TPU:8, one launch (start us, length us, event | category | flops | bytes accessed | tf_op | source)
XLA Modules:
  0.0 572.4 jit_solution(15767024178187781781)
XLA Ops:
  7.1 12.3 %all-to-all-start = ((bf16[64,128,256]{2,1,0:T(8,128)(2,1)}), bf16[64,128,256]{2,1,0:T(8,128)(2,1)}, u32[]{:S(2)}, u32[]{:S(2)}) async-start(bf16[64,128,256]{2,1,0:T(8,128)(2,1)} %gather_fusion), calls=%async_computation | async-start | bytes 8388608 | tf_op jit(solution)/shard_map/all_to_all | solution.py:53
  21.4 94.3 %all-to-all-done = bf16[64,128,256]{2,1,0:T(8,128)(2,1)} async-done(((bf16[64,128,256]{2,1,0:T(8,128)(2,1)}), bf16[64,128,256]{2,1,0:T(8,128)(2,1)}, u32[]{:S(2)}, u32[]{:S(2)}) %all-to-all-start) | async-done | bytes 4194336 | tf_op jit(solution)/shard_map/all_to_all | solution.py:53
  117.0 5.2 all-to-all-start.2
  122.2 4.6 pad_maximum_fusion
  126.9 10.9 %gather_fusion.1 = bf16[201,128,256]{2,1,0:T(8,128)(2,1)} fusion(bf16[70,128,256]{2,1,0:T(8,128)(2,1)} %pad_maximum_fusion, s32[1024]{0:T(1024)S(1)} %pad_clamp_fusion), kind=kCustom, calls=%fused_computation.1 | custom fusion | bytes 26346276 | tf_op jit(solution)/shard_map/gather | solution.py:55
  137.8 16.7 %convolution_bitcast_fusion.1 = f32[201,128,256]{1,2,0:T(8,128)} fusion(bf16[201,128,256]{2,1,0:T(8,128)(2,1)} %gather_fusion.1, bf16[1,201,128,128]{3,2,1,0:T(8,128)(2,1)} %param.16), kind=kOutput, calls=%fused_computation.5 | convolution fusion | flops 1686110208 | bytes 46104576 | tf_op jit(solution)/shard_map/tij,tjc->tic/dot_general | solution.py:56
  154.5 27.1 %copy.38 = f32[201,128,256]{2,0,1:T(8,128)} copy(f32[201,128,256]{1,2,0:T(8,128)} %convolution_bitcast_fusion.1) | data formatting | bytes 52690944 | tf_op jit(solution)/shard_map/tij,tjc->tic/dot_general | solution.py:56
  181.5 13.2 %multiply_convert_fusion = (bf16[6,128,256]{2,0,1:T(8,128)(2,1)S(1)}, f32[6,128,256]{2,0,1:T(8,128)S(1)}) fusion(f32[6,128]{0,1:T(8,128)S(1)} %copy-done.6, f32[201,128,256]{2,0,1:T(8,128)} %copy.38, s32[201]{0:T(256)S(1)} %bitcast.66, pred[201]{0:T(512)(128)(4,1)S(1)} %copy-done.10), kind=kOutput, calls=%fused_computation.13 | convolution fusion | flops 474810752 | bytes 27529196 | tf_op jit(solution)/shard_map/tr,tic->ric/dot_general | solution.py:59
  198.8 10.7 %all-to-all-start.1 = ((bf16[64,128,256]{2,1,0:T(8,128)(2,1)}), bf16[64,128,256]{2,1,0:T(8,128)(2,1)}, u32[]{:S(2)}, u32[]{:S(2)}) async-start(bf16[64,128,256]{2,1,0:T(8,128)(2,1)} %gather_fusion.2), calls=%async_computation.1 | async-start | bytes 8388608 | tf_op jit(solution)/shard_map/all_to_all | solution.py:53
  212.1 2.9 reshape.196
  215.2 90.5 %all-to-all-done.1 = bf16[64,128,256]{2,1,0:T(8,128)(2,1)} async-done(((bf16[64,128,256]{2,1,0:T(8,128)(2,1)}), bf16[64,128,256]{2,1,0:T(8,128)(2,1)}, u32[]{:S(2)}, u32[]{:S(2)}) %all-to-all-start.1) | async-done | bytes 4194336 | tf_op jit(solution)/shard_map/all_to_all | solution.py:53
  305.7 4.6 pad_maximum_fusion.1
  310.3 10.9 %gather_fusion.3 = bf16[201,128,256]{2,1,0:T(8,128)(2,1)} fusion(bf16[70,128,256]{2,1,0:T(8,128)(2,1)} %pad_maximum_fusion.1, s32[1024]{0:T(1024)S(1)} %pad_clamp_fusion), kind=kCustom, calls=%fused_computation.3 | custom fusion | bytes 26346276 | tf_op jit(solution)/shard_map/gather | solution.py:55
  321.2 16.7 %convolution_bitcast_fusion = f32[201,128,256]{1,2,0:T(8,128)} fusion(bf16[201,128,256]{2,1,0:T(8,128)(2,1)} %gather_fusion.3, bf16[1,201,128,128]{3,2,1,0:T(8,128)(2,1)} %param.16), kind=kOutput, calls=%fused_computation.4 | convolution fusion | flops 1686110208 | bytes 46104576 | tf_op jit(solution)/shard_map/tij,tjc->tic/dot_general | solution.py:56
  337.9 27.0 %copy.44 = f32[201,128,256]{2,0,1:T(8,128)} copy(f32[201,128,256]{1,2,0:T(8,128)} %convolution_bitcast_fusion) | data formatting | bytes 52690944 | tf_op jit(solution)/shard_map/tij,tjc->tic/dot_general | solution.py:56
  364.9 13.2 %fusion.8 = f32[6,128,256]{2,0,1:T(8,128)S(1)} fusion(f32[201,128,256]{2,0,1:T(8,128)} %copy.44, s32[201]{0:T(256)S(1)} %bitcast.67, pred[201]{0:T(512)(128)(4,1)S(1)} %copy-done.11), kind=kOutput, calls=%fused_computation.27 | convolution fusion | flops 474220928 | bytes 27132908 | tf_op jit(solution)/shard_map/tr,tic->ric/dot_general | solution.py:59
  386.5 39.5 %all_to_all.30 = f32[4,192,1024]{2,1,0:T(8,128)S(1)} all-to-all(f32[4,192,1024]{2,1,0:T(8,128)S(1)} %fusion.18), channel_id=1, replica_groups=mesh['node_0'=8,'node_1'=4,'node_2'=2,'feat'=4] {'feat'}, dimensions={0} | all-to-all | bytes 6291456 | tf_op jit(solution)/shard_map/all_to_all | solution.py:38
  430.9 5.0 all-to-all-start.4
  437.5 15.4 %all-to-all-done.4 = bf16[4,192,1024]{2,1,0:T(8,128)(2,1)S(1)} async-done(((bf16[4,192,1024]{2,1,0:T(8,128)(2,1)}), bf16[4,192,1024]{2,1,0:T(8,128)(2,1)S(1)}, u32[]{:S(2)}, u32[]{:S(2)}) %all-to-all-start.4) | async-done | bytes 1572896 | tf_op jit(solution)/shard_map/all_to_all | solution.py:14
  454.5 4.8 fusion.2
  459.3 9.0 %all-to-all-start.5 = ((f32[64,16,3,256]{3,1,2,0:T(8,128)}), f32[64,16,3,256]{3,1,2,0:T(8,128)S(1)}, u32[]{:S(2)}, u32[]{:S(2)}) async-start(f32[64,16,3,256]{3,1,2,0:T(8,128)} %fusion.2), calls=%async_computation.5 | async-start | bytes 6291456 | tf_op jit(solution)/shard_map/all_to_all | solution.py:38
  468.3 80.4 %psum.28 = f32[1024]{0:T(1024)S(1)} all-reduce(f32[1024]{0:T(1024)S(1)} %get-tuple-element.3), channel_id=1, replica_groups=mesh['node_0'=8,'node_1'=4,'node_2'=2,'feat'=4] {'node_0'}, use_global_device_ids=true, to_apply=%region_3.4 | all-reduce | flops 1024 | bytes 8192 | tf_op jit(solution)/shard_map/psum | solution.py:44
  548.7 10.7 %psum.29 = f32[1024]{0:T(1024)S(1)} all-reduce(f32[1024]{0:T(1024)S(1)} %psum.28), channel_id=1, replica_groups=mesh['node_0'=8,'node_1'=4,'node_2'=2,'feat'=4] {'node_1'}, use_global_device_ids=true, to_apply=%region_4.5 | all-reduce | flops 1024 | bytes 8192 | tf_op jit(solution)/shard_map/psum | solution.py:44
  561.9 9.7 %psum.31 = f32[1024]{0:T(1024)} all-reduce(f32[1024]{0:T(1024)S(1)} %psum.30), channel_id=1, replica_groups=mesh['node_0'=8,'node_1'=4,'node_2'=2,'feat'=4] {'feat'}, use_global_device_ids=true, to_apply=%region_6.7 | all-reduce | flops 1024 | bytes 8192 | tf_op jit(solution)/shard_map/psum | solution.py:44
  (55 shorter events, 35.5 us)
Async XLA Ops:
  7.1 14.2 %copy-start.12 = (s32[1,201]{1,0:T(1,128)S(1)}, s32[1,201]{1,0:T(1,128)}, u32[]{:S(2)}) copy-start(s32[1,201]{1,0:T(1,128)} %param.13) | copy-start | bytes 2416
  7.1 108.6 %copy-start.7 = (bf16[16,3,256]{2,0,1:T(8,128)(2,1)S(1)}, bf16[16,3,256]{2,0,1:T(8,128)(2,1)}, u32[]{:S(2)}) copy-start(bf16[16,3,256]{2,0,1:T(8,128)(2,1)} %param.17) | copy-start | bytes 73732
  7.1 108.6 %all-to-all-start = ((bf16[64,128,256]{2,1,0:T(8,128)(2,1)}), bf16[64,128,256]{2,1,0:T(8,128)(2,1)}, u32[]{:S(2)}, u32[]{:S(2)}) async-start(bf16[64,128,256]{2,1,0:T(8,128)(2,1)} %gather_fusion), calls=%async_computation | async-start | bytes 8388608 | tf_op jit(solution)/shard_map/all_to_all | solution.py:53
  117.0 80.6 %all-to-all-start.2 = ((bf16[64,16,3,256]{3,1,2,0:T(8,128)(2,1)}), bf16[64,16,3,256]{3,1,2,0:T(8,128)(2,1)S(1)}, u32[]{:S(2)}, u32[]{:S(2)}) async-start(bf16[64,16,3,256]{3,1,2,0:T(8,128)(2,1)} %broadcast_in_dim.4), calls=%async_computation.2 | async-start | bytes 3145728 | tf_op jit(solution)/shard_map/all_to_all | solution.py:14
  154.5 27.1 %copy-start.6 = (f32[6,128]{0,1:T(8,128)S(1)}, f32[6,128]{0,1:T(8,128)}, u32[]{:S(2)}) copy-start(f32[6,128]{0,1:T(8,128)} %copy.40) | copy-start | bytes 9220
  154.5 27.1 %copy-start.8 = (s32[1,201]{1,0:T(1,128)S(1)}, s32[1,201]{1,0:T(1,128)}, u32[]{:S(2)}) copy-start(s32[1,201]{1,0:T(1,128)} %param.12) | copy-start | bytes 2416
  154.5 27.1 %copy-start.10 = (pred[201]{0:T(512)(128)(4,1)S(1)}, pred[201]{0:T(512)(128)(4,1)}, u32[]{:S(2)}) copy-start(pred[201]{0:T(512)(128)(4,1)} %iota_compare_fusion.1) | copy-start | bytes 607
  197.6 1.2 copy-start.2
  198.8 106.9 %all-to-all-start.1 = ((bf16[64,128,256]{2,1,0:T(8,128)(2,1)}), bf16[64,128,256]{2,1,0:T(8,128)(2,1)}, u32[]{:S(2)}, u32[]{:S(2)}) async-start(bf16[64,128,256]{2,1,0:T(8,128)(2,1)} %gather_fusion.2), calls=%async_computation.1 | async-start | bytes 8388608 | tf_op jit(solution)/shard_map/all_to_all | solution.py:53
  337.9 27.0 %copy-start.11 = (pred[201]{0:T(512)(128)(4,1)S(1)}, pred[201]{0:T(512)(128)(4,1)}, u32[]{:S(2)}) copy-start(pred[201]{0:T(512)(128)(4,1)} %iota_compare_fusion.1) | copy-start | bytes 607
  378.1 1.0 copy-start.4
  378.6 5.2 copy-start.3
  379.3 1.0 copy-start
  386.5 40.7 %copy-start.5 = (bf16[192,1024]{1,0:T(8,128)(2,1)S(1)}, bf16[192,1024]{1,0:T(8,128)(2,1)}, u32[]{:S(2)}) copy-start(bf16[192,1024]{1,0:T(8,128)(2,1)} %param.19) | copy-start | bytes 1179652
  386.5 40.7 %copy-start.9 = (f32[1024]{0:T(1024)S(1)}, f32[1024]{0:T(1024)}, u32[]{:S(2)}) copy-start(f32[1024]{0:T(1024)} %param.18) | copy-start | bytes 12292
  427.2 8.7 %copy-start.1 = (bf16[768,3,256]{2,0,1:T(8,128)(2,1)S(1)}, bf16[768,3,256]{2,0,1:T(8,128)(2,1)}, u32[]{:S(2)}) copy-start(bf16[768,3,256]{2,0,1:T(8,128)(2,1)} %copy-done) | copy-start | bytes 3538948
  430.9 22.0 %all-to-all-start.4 = ((bf16[4,192,1024]{2,1,0:T(8,128)(2,1)}), bf16[4,192,1024]{2,1,0:T(8,128)(2,1)S(1)}, u32[]{:S(2)}, u32[]{:S(2)}) async-start(bf16[4,192,1024]{2,1,0:T(8,128)(2,1)} %broadcast_in_dim.5), calls=%async_computation.4 | async-start | bytes 3145728 | tf_op jit(solution)/shard_map/all_to_all | solution.py:14
  459.3 112.3 %all-to-all-start.5 = ((f32[64,16,3,256]{3,1,2,0:T(8,128)}), f32[64,16,3,256]{3,1,2,0:T(8,128)S(1)}, u32[]{:S(2)}, u32[]{:S(2)}) async-start(f32[64,16,3,256]{3,1,2,0:T(8,128)} %fusion.2), calls=%async_computation.5 | async-start | bytes 6291456 | tf_op jit(solution)/shard_map/all_to_all | solution.py:38
where the time goes:
time: 574 us; the launch traced here: 572 us
  waiting for transfers between devices  200 us (35%)
  blocking collectives  143 us (25%)
  local copies, waits for them, and re-layouts  100 us (17%)
  matrix products  67.3 us (12%)
  starting transfers between devices  42.3 us (7%)
  other arithmetic  18.2 us (3%)
    all_to_all x2, waiting for transfers between devices, propagate(): lax.all_to_all(outgoing, NODE, split_axis=0, concat_axis=0, tiled=True)  185 us
    psum x4, blocking collectives, over_axes(): shard = lax.psum(shard, axis)  103 us
    dot_general x2, local copies, waits for them, and re-layouts, propagate(): jnp.einsum('tij,tjc->tic', tile_values, sources, preferred_element_type=j...  54.1 us
    all_to_all x1, blocking collectives, sum_at_owner(): lax.all_to_all(split_up(shard, dim, devices), axis, 0, 0, tiled=True)  39.5 us
    dot_general x2, matrix products, propagate(): jnp.einsum('tij,tjc->tic', tile_values, sources, preferred_element_type=j...  33.4 us
    dot_general x2, matrix products, propagate(): jnp.einsum('tr,tic->ric', onehot, product, precision=lax.Precision.HIGHEST)  26.4 us
    all_to_all x2, starting transfers between devices, propagate(): lax.all_to_all(outgoing, NODE, split_axis=0, concat_axis=0, tiled=True)  23.1 us
    gather x2, local copies, waits for them, and re-layouts, propagate(): sources = frame[tile_cols]  21.8 us
  transfers between devices with their start and end apart: 5, of which 3 were waited for; matrix products, arithmetic and copies ran while one was open for 15% of the time, Pallas kernels for 0%

commit v1 on v0

v1 whole, which is shorter than its diff:
```python
import functools

import jax
import jax.numpy as jnp
from jax import lax
from jax.experimental import pallas as pl
from jax.experimental.pallas import tpu as pltpu
from jax.sharding import Mesh
from jax.sharding import PartitionSpec as P

HOPS = 2
GROUP = 8
Z = "node_0"
XC = ("node_1", "node_2")
NODE = ("node_0", "node_1", "node_2")
NODE_FEAT = ("node_0", "node_1", "node_2", "feat")


def dense_body(rows, slots, count, values, out):
    block = values.shape[-1]

    def clear(slot, carry):
        out[slot] = jnp.zeros_like(out[slot])
        return carry

    lax.fori_loop(0, out.shape[0], clear, 0)

    def step(tile, carry):
        place = (slots[tile], pl.ds(pl.multiple_of(rows[tile] * block, block), block), slice(None))
        out[place] = out[place] + values[tile]
        return carry

    lax.fori_loop(0, count[0], step, 0)


def densify(tile_rows, slots, count, tile_values, slot_total, row_total):
    block = tile_values.shape[-1]
    smem = pl.BlockSpec(memory_space=pltpu.SMEM)
    return pl.pallas_call(
        dense_body,
        out_shape=jax.ShapeDtypeStruct((slot_total, row_total, block), tile_values.dtype),
        in_specs=[smem, smem, smem, pl.BlockSpec(memory_space=pltpu.VMEM)],
        out_specs=pl.BlockSpec(memory_space=pltpu.VMEM),
        compiler_params=pltpu.CompilerParams(vmem_limit_bytes=40 << 20),
        name="densify",
    )(tile_rows, slots, count, tile_values)


def pick_body(places, wanted, *refs):
    sources, out = refs[:-1], refs[-1]
    for number, place in enumerate(places):
        for target in range(out.shape[0]):
            out[target, number] = sources[number][wanted[place, target]]


def pick(places, wanted, sources):
    block, width = sources[0].shape[1:]
    vmem = pl.BlockSpec(memory_space=pltpu.VMEM)
    return pl.pallas_call(
        functools.partial(pick_body, places),
        out_shape=jax.ShapeDtypeStruct(
            (wanted.shape[1], len(places), block, width), sources[0].dtype
        ),
        in_specs=[pl.BlockSpec(memory_space=pltpu.SMEM)] + [vmem] * len(sources),
        out_specs=vmem,
        compiler_params=pltpu.CompilerParams(vmem_limit_bytes=16 << 20),
        name="pick",
    )(wanted, *sources)


def hop_stage(dense, base, own, arrived, summed, scale):
    row_total, block = dense.shape[1:]
    width = arrived.shape[-1]
    last = scale is not None
    lead = 0 if own is None else 1

    def body(*refs):
        tiles, refs = refs[0], refs[1:]
        if lead:
            mine, refs = refs[0], refs[1:]
        sources, refs = refs[0], refs[1:]
        if summed is not None:
            before, refs = refs[0], refs[1:]
        if last:
            scaling, hop, source, acc = refs
        else:
            (acc,) = refs

        def product(right):
            size = right.shape[0] // block
            left = jnp.concatenate([tiles[i] for i in range(size)], axis=1)
            return jnp.dot(left, right, preferred_element_type=jnp.float32)

        step = pl.program_id(0)
        if lead:

            @pl.when(step == 0)
            def _():
                acc[...] = product(mine[...].reshape(-1, width))

        else:

            @pl.when(step == 0)
            def _():
                acc[...] = before[...]

        @pl.when(step >= lead)
        def _():
            acc[...] += product(sources[...].reshape(-1, width))

        if last:

            @pl.when(step == pl.num_programs(0) - 1)
            def _():
                scaled = acc[...] * scaling[...]
                hop[...] = scaled.astype(hop.dtype)
                source[...] = (scaled * scaling[...]).astype(source.dtype)

    flat = pl.BlockSpec((row_total, width), lambda i: (0, 0))
    operands, in_specs = [dense], [pl.BlockSpec((GROUP, row_total, block), lambda i: (base + i, 0, 0))]
    if lead:
        operands.append(own)
        in_specs.append(pl.BlockSpec(own.shape, lambda i: (0, 0, 0)))
    operands.append(arrived)
    in_specs.append(
        pl.BlockSpec((arrived.shape[0], 1, block, width), lambda i: (0, jnp.maximum(i - lead, 0), 0, 0))
    )
    if summed is not None:
        operands.append(summed)
        in_specs.append(flat)
    total = jax.ShapeDtypeStruct((row_total, width), jnp.float32)
    rounded = jax.ShapeDtypeStruct((row_total, width), jnp.bfloat16)
    if last:
        operands.append(scale)
        in_specs.append(flat)
    return pl.pallas_call(
        body,
        grid=(arrived.shape[1] + lead,),
        out_shape=(rounded, rounded) if last else total,
        in_specs=in_specs,
        out_specs=(flat, flat) if last else flat,
        scratch_shapes=[pltpu.VMEM((row_total, width), jnp.float32)] if last else [],
        compiler_params=pltpu.CompilerParams(vmem_limit_bytes=40 << 20),
        name="hop_last" if last else "hop_stage",
    )(*operands)


def shift(array, axis, step):
    length = lax.axis_size(axis)
    return lax.ppermute(array, axis, [(i, (i + step) % length) for i in range(length)])


def propagate(source, dense, wanted, scale, block):
    _, width = source.shape
    along = lax.axis_size(Z)
    own = source.reshape(-1, block, width)
    half = own.shape[0] // 2

    def exchange(places, sources):
        outgoing = pick(places, wanted, sources)
        return lax.all_to_all(outgoing, XC, split_axis=0, concat_axis=0, tiled=True)

    arrived = [exchange([0], [own])]
    low, high = own, own
    far = along // 2
    for distance in range(1, far):
        low, high = shift(low, Z, 1), shift(high, Z, -1)
        if distance < far - 1:
            arrived.append(exchange([distance, along - distance], [high, low]))
    opposite = [shift(low[:half], Z, 1), shift(high[half:], Z, -1)]
    opposite = jnp.concatenate(opposite, axis=0)
    places = [far - 1, along - far + 1, far]
    arrived.append(exchange(places, [high, low, opposite]))
    summed = hop_stage(dense, 0, own, arrived[0], None, None)
    summed = hop_stage(dense, 2, None, arrived[1], summed, None)
    summed = hop_stage(dense, 4, None, arrived[2], summed, None)
    return hop_stage(dense, 6, None, arrived[3], summed, scale)


def at(array, index):
    return lax.dynamic_index_in_dim(array, index % array.shape[0], 0, keepdims=False)


def ring_sum(pieces, axis):
    opposite, following, leading, mine = pieces
    half = opposite.shape[0] // 2
    opposite = opposite.astype(jnp.bfloat16)
    up, down = shift(opposite[:half], axis, 1), shift(opposite[half:], axis, -1)
    up, down = up.astype(jnp.float32), down.astype(jnp.float32)
    following = jnp.concatenate([following[:half] + up, following[half:]]).astype(jnp.bfloat16)
    leading = jnp.concatenate([leading[:half], leading[half:] + down]).astype(jnp.bfloat16)
    up, down = shift(following, axis, 1), shift(leading, axis, -1)
    return mine + up.astype(jnp.float32) + down.astype(jnp.float32)


def layer(features, hops, flat_weight, weight, out_bias, cotangent):
    rows, along = features.shape[0], lax.axis_size(Z)
    panels = lax.axis_size("feat")
    feat_index = lax.axis_index("feat")
    flat_rows = jnp.concatenate([features.astype(jnp.bfloat16)] + hops, axis=1)
    by_owner = flat_rows.reshape(panels, rows // panels, -1)
    near = [at(by_owner, feat_index + i) for i in range(panels)]

    def term_of(owner_rows):
        return lax.dot_general(
            owner_rows, flat_weight, (((1,), (1,)), ((), ())), preferred_element_type=jnp.float32
        )

    linear = ring_sum([term_of(near[2]), term_of(near[1]), term_of(near[3]), term_of(near[0])], "feat")
    linear = linear + out_bias[None, :]
    sigmoid_val = jax.nn.sigmoid(linear)
    output = (linear * sigmoid_val).astype(jnp.bfloat16)
    grad_linear = (
        cotangent.astype(jnp.float32) * sigmoid_val * (1.0 + linear * (1.0 - sigmoid_val))
    ).astype(jnp.bfloat16)

    bias = jnp.sum(grad_linear.astype(jnp.float32), axis=0)
    for axes in (("node_1", "node_2", "feat"), Z):
        copies = jnp.broadcast_to(bias[None], (lax.axis_size(axes), bias.shape[0]))
        copies = lax.all_to_all(copies, axes, 0, 0, tiled=True)
        bias = jnp.sum(copies, axis=0)

    half = grad_linear.shape[0] // 2
    up, down = shift(grad_linear, "feat", 1), shift(grad_linear, "feat", -1)
    opposite = [shift(up[:half], "feat", 1), shift(down[half:], "feat", -1)]
    opposite = jnp.concatenate(opposite)

    def outer(grads, owner_rows):
        return lax.dot_general(
            grads, owner_rows, (((0,), (0,)), ((), ())), preferred_element_type=jnp.float32
        )

    term = outer(jnp.concatenate([grad_linear, up, down]), jnp.concatenate([near[0], near[3], near[1]]))
    term = term + outer(opposite, near[2])
    columns = term.shape[1]
    term = term.reshape(along, 4, 2, weight.shape[0], columns)
    term = jnp.moveaxis(term, (2, 1), (0, 1))
    core = lax.axis_index("node_2")
    other = shift(at(term, core + 1).astype(jnp.bfloat16), "node_2", 1)
    term = (at(term, core) + other.astype(jnp.float32)).reshape(4, -1, columns)
    x_index = lax.axis_index("node_1")
    term = ring_sum([at(term, x_index + i) for i in (2, 1, 3, 0)], "node_1")
    term = term.astype(jnp.bfloat16).reshape(along, -1, columns)
    term = lax.all_to_all(term, Z, 0, 0, tiled=True)
    weight_grad = jnp.sum(term.astype(jnp.float32), axis=0).reshape(weight.shape)
    return (output, weight_grad, bias)


def local(
    features,
    degrees,
    tile_row,
    tile_col,
    tile_count,
    send_block,
    tile_val,
    weight,
    out_bias,
    cotangent,
):
    rows, panel = features.shape
    block = tile_val.shape[-1]
    row_blocks = rows // block
    parts = send_block.shape[0]
    along = lax.axis_size(Z)
    across = parts // along
    z_index = lax.axis_index(Z)
    xc_index = lax.axis_index(XC)

    flat_weight = lax.all_gather(weight.reshape(weight.shape[0], -1), NODE, axis=0, tiled=True)
    row_scale = lax.rsqrt(degrees.astype(jnp.float32))[:, None]
    source = (features * row_scale).astype(jnp.bfloat16)
    scale = jnp.broadcast_to(row_scale, (rows, panel))

    by_place = send_block.reshape(along, across, along, across)
    mine = lax.dynamic_index_in_dim(by_place, xc_index, 1, keepdims=False)
    mine = lax.dynamic_index_in_dim(mine, z_index, 1, keepdims=False)
    wanted = jnp.roll(mine, -z_index, axis=0)

    order = [0]
    for distance in range(1, along // 2):
        order += [distance, along - distance]
    order.append(along // 2)
    place_of = jnp.array([order.index(offset) for offset in range(along)], dtype=jnp.int32)
    sender = jnp.maximum(tile_col[0] - row_blocks, 0)
    offset = (sender // across - z_index) % along
    remote = GROUP + place_of[offset] * across + sender % across
    slots = jnp.where(tile_col[0] < row_blocks, tile_col[0], remote)
    dense = densify(tile_row[0], slots, tile_count, tile_val[0], GROUP + parts, rows)

    hops = []
    for _ in range(HOPS):
        hop, source = propagate(source, dense, wanted, scale, block)
        hops.append(hop)

    args = (features, hops, flat_weight, weight, out_bias, cotangent)
    return layer(*args)


def solution(mesh):
    split = Mesh(
        mesh.devices.reshape(8, 4, 2, mesh.shape["feat"]), ("node_0", "node_1", "node_2", "feat")
    )
    return jax.shard_map(
        local,
        mesh=split,
        in_specs=(
            P(NODE, "feat"),
            P(NODE),
            P(NODE, None),
            P(NODE, None),
            P(NODE),
            P(),
            P(NODE, None, None, None),
            P(NODE, None, "feat"),
            P(),
            P(NODE_FEAT, None),
        ),
        out_specs=(P(NODE_FEAT, None), P(NODE, None, "feat"), P()),
        check_vma=False,
    )
```

time: 574 us -> 332 us (0.58)
  blocking collectives: 143 us -> 0 us
  local copies, waits for them, and re-layouts: 100 us -> 22.4 us
  matrix products: 67.3 us -> 6.13 us
  waiting for transfers between devices: 200 us -> 141 us
  starting transfers between devices: 42.3 us -> 94.5 us
  Pallas kernels: 0 us -> 43.8 us
  between operations: 1.43 us -> 15.4 us
  other arithmetic: 18.2 us -> 7.78 us
    all_to_all x5 -> x11, waiting for transfers between devices: 200 us -> 38.6 us  [the longest x8 15.8 us: exchange(): return lax.all_to_all(outgoing, XC, split_axis=0, concat_axis=0, tiled=True)]
    psum x4 -> x0, blocking collectives: 103 us -> none  [over_axes(): shard = lax.psum(shard, axis)]
    ppermute x0 -> x29, waiting for transfers between devices: none -> 101 us  [shift(): lax.ppermute(array, axis, [(i, (i + step) % length) for i in range(length)])]
    dot_general x6, matrix products: 67.3 us -> 6.13 us  [the longest x4 4.04 us: term_of(): lax.dot_general(owner_rows, flat_weight, (((1,), (1,)), ((), ())), prefer...]
    dot_general x6 -> x0, local copies, waits for them, and re-layouts: 58.6 us -> none  [the longest x2 54.1 us: propagate(): jnp.einsum('tij,tjc->tic', tile_values, sources, preferred_element_type=j...]
    ppermute x0 -> x29, starting transfers between devices: none -> 45.9 us  [shift(): lax.ppermute(array, axis, [(i, (i + step) % length) for i in range(length)])]
    pallas_call x0 -> x17, Pallas kernels: none -> 43.8 us  [the longest x8 25.1 us: hop_stage(): pl.pallas_call(body, grid=(arrived.shape[1] + lead,), out_shape=(rounded,...]
    all_to_all x1 -> x0, blocking collectives: 39.5 us -> none  [sum_at_owner(): lax.all_to_all(split_up(shard, dim, devices), axis, 0, 0, tiled=True)]
  transfers between devices with their start and end apart: 5 -> 41, of which waited for: 3 -> 26; matrix products, arithmetic and copies ran while one was open for 15% -> 2% of each run, Pallas kernels for 0% -> 11%
where the time goes in v1:
time: 332 us; the launch traced here: 331 us
  waiting for transfers between devices  141 us (42%)
  starting transfers between devices  94.5 us (28%)
  Pallas kernels  43.8 us (13%)
  local copies, waits for them, and re-layouts  22.4 us (7%)
  between operations  15.4 us (5%)
  other arithmetic  7.78 us (2%)
  matrix products  6.13 us (2%)
    ppermute x29, waiting for transfers between devices, shift(): lax.ppermute(array, axis, [(i, (i + step) % length) for i in range(length)])  101 us
    ppermute x29, starting transfers between devices, shift(): lax.ppermute(array, axis, [(i, (i + step) % length) for i in range(length)])  45.9 us
    all_to_all x8, starting transfers between devices, exchange(): return lax.all_to_all(outgoing, XC, split_axis=0, concat_axis=0, tiled=True)  32.8 us
    pallas_call x8, Pallas kernels, hop_stage(): pl.pallas_call(body, grid=(arrived.shape[1] + lead,), out_shape=(rounded,...  25.1 us
    unnamed x60, local copies, waits for them, and re-layouts  18.4 us
    all_to_all x8, waiting for transfers between devices, exchange(): return lax.all_to_all(outgoing, XC, split_axis=0, concat_axis=0, tiled=True)  15.8 us
    all_to_all x2, waiting for transfers between devices, layer(): copies = lax.all_to_all(copies, axes, 0, 0, tiled=True)  13.7 us
    all_to_all x2, starting transfers between devices, layer(): copies = lax.all_to_all(copies, axes, 0, 0, tiled=True)  12.4 us
  transfers between devices with their start and end apart: 41, of which 26 were waited for; matrix products, arithmetic and copies ran while one was open for 2% of the time, Pallas kernels for 11%

profile of v1, /device:TPU:8, one launch (start us, length us, event | category | flops | bytes accessed | tf_op | source)
XLA Modules:
  0.0 330.7 jit_solution(15613093561876457131)
XLA Ops:
  12.6 4.3 %all-to-all-start.3 = ((bf16[8,1,128,256]{3,2,1,0:T(8,128)(2,1)}), bf16[8,1,128,256]{3,2,1,0:T(8,128)(2,1)S(1)}, u32[]{:S(2)}, u32[]{:S(2)}) async-start(bf16[8,1,128,256]{3,2,1,0:T(8,128)(2,1)} %pick.11), calls=%async_computation.3 | async-start | bytes 1048576 | tf_op jit(solution)/shard_map/all_to_all | solution.py:161
  16.9 5.9 %collective-permute-start = (bf16[6,128,256]{2,1,0:T(8,128)(2,1)S(1)}, bf16[6,128,256]{2,1,0:T(8,128)(2,1)S(1)}, u32[]{:S(2)}, u32[]{:S(2)}) collective-permute-start(bf16[6,128,256]{2,1,0:T(8,128)(2,1)S(1)} %bitcast.83), channel_id=1, source_target_pairs={{0,224},{32,0},{64,32},{96,64},{128,96},{160,128},{192,160},{224,1... | collective-permute-start | bytes 1179656 | tf_op jit(solution)/shard_map/ppermute | solution.py:150
  22.7 9.0 %collective-permute-done.refs_0_ = bf16[6,128,256]{2,1,0:T(8,128)(2,1)S(1)} collective-permute-done((bf16[6,128,256]{2,1,0:T(8,128)(2,1)S(1)}, bf16[6,128,256]{2,1,0:T(8,128)(2,1)S(1)}, u32[]{:S(2)}, u32[]{:S(2)}) %collective-permute-start) | collective-permute-done | bytes 393248 | tf_op jit(solution)/shard_map/ppermute | solution.py:150
  36.8 4.4 %all-to-all-start.2 = ((bf16[8,2,128,256]{3,2,1,0:T(8,128)(2,1)}), bf16[8,2,128,256]{3,2,1,0:T(8,128)(2,1)S(1)}, u32[]{:S(2)}, u32[]{:S(2)}) async-start(bf16[8,2,128,256]{3,2,1,0:T(8,128)(2,1)} %pick.10), calls=%async_computation.2 | async-start | bytes 2097152 | tf_op jit(solution)/shard_map/all_to_all | solution.py:161
  43.3 9.5 %collective-permute-done.1.refs_0_ = bf16[6,128,256]{2,1,0:T(8,128)(2,1)S(1)} collective-permute-done((bf16[6,128,256]{2,1,0:T(8,128)(2,1)S(1)}, bf16[6,128,256]{2,1,0:T(8,128)(2,1)S(1)}, u32[]{:S(2)}, u32[]{:S(2)}) %collective-permute-start.1) | collective-permute-done | bytes 393248 | tf_op jit(solution)/shard_map/ppermute | solution.py:150
  64.1 9.7 %collective-permute-done.5.refs_1_ = bf16[6,128,256]{2,1,0:T(8,128)(2,1)S(1)} collective-permute-done((bf16[6,128,256]{2,1,0:T(8,128)(2,1)}, bf16[6,128,256]{2,1,0:T(8,128)(2,1)S(1)}, u32[]{:S(2)}, u32[]{:S(2)}) %collective-permute-start.5) | collective-permute-done | bytes 393248 | tf_op jit(solution)/shard_map/ppermute | solution.py:150
  77.2 4.3 %collective-permute-done.6 = bf16[3,128,256]{2,1,0:T(8,128)(2,1)S(1)} collective-permute-done((bf16[3,128,256]{2,1,0:T(8,128)(2,1)S(1)}, bf16[3,128,256]{2,1,0:T(8,128)(2,1)S(1)}, u32[]{:S(2)}, u32[]{:S(2)}) %collective-permute-start.6) | collective-permute-done | bytes 196640 | tf_op jit(solution)/shard_map/ppermute | solution.py:150
  92.1 8.7 %densify.1.refs_0_ = bf16[72,768,128]{2,1,0:T(8,128)(2,1)} custom-call(s32[201]{0:T(256)S(1)} %bitcast.90, s32[201]{0:T(256)S(1)} %compare_select_fusion.9.slots, s32[1]{0:T(128)S(6)} %copy.43.count, bf16[201,128,128]{2,1,0:T(8,128)(2,1)S(1)} %bitcast.81), custom_call_target="tpu_custom_call" | custom-call | tf_op jit(solution)/shard_map/densify/pallas_call | solution.py:39
  110.2 4.2 %hop_last.2 = (bf16[768,256]{1,0:T(8,128)(2,1)S(1)}, bf16[768,256]{1,0:T(8,128)(2,1)S(1)}) custom-call(bf16[72,768,128]{2,1,0:T(8,128)(2,1)} %densify.1.refs_0_, bf16[8,3,128,256]{3,2,1,0:T(8,128)(2,1)S(1)} %all-to-all-done.refs_1_, f32[768,256]{1,0:T(8,128)S(1)} %hop_stage.8.refs_2_, f32[768,256]{1,0:T(8,128)S(1)} %mul.28.refs_3_), custom_call_target="tpu_custom_call" | custom-call | tf_op jit(solution)/shard_map/hop_last/pallas_call | solution.py:136
  123.7 9.6 %collective-permute-done.11.refs_1_ = bf16[6,128,256]{2,1,0:T(8,128)(2,1)S(1)} collective-permute-done((bf16[6,128,256]{2,1,0:T(8,128)(2,1)}, bf16[6,128,256]{2,1,0:T(8,128)(2,1)S(1)}, u32[]{:S(2)}, u32[]{:S(2)}) %collective-permute-start.11) | collective-permute-done | bytes 393248 | tf_op jit(solution)/shard_map/ppermute | solution.py:150
  135.8 4.4 %all-to-all-start.6 = ((bf16[8,2,128,256]{3,2,1,0:T(8,128)(2,1)}), bf16[8,2,128,256]{3,2,1,0:T(8,128)(2,1)S(1)}, u32[]{:S(2)}, u32[]{:S(2)}) async-start(bf16[8,2,128,256]{3,2,1,0:T(8,128)(2,1)} %pick.14), calls=%async_computation.6 | async-start | bytes 2097152 | tf_op jit(solution)/shard_map/all_to_all | solution.py:161
  144.3 9.7 %collective-permute-done.12.refs_1_ = bf16[6,128,256]{2,1,0:T(8,128)(2,1)S(1)} collective-permute-done((bf16[6,128,256]{2,1,0:T(8,128)(2,1)S(1)}, bf16[6,128,256]{2,1,0:T(8,128)(2,1)S(1)}, u32[]{:S(2)}, u32[]{:S(2)}) %collective-permute-start.12) | collective-permute-done | bytes 393248 | tf_op jit(solution)/shard_map/ppermute | solution.py:150
  156.4 4.4 %all-to-all-start.5 = ((bf16[8,2,128,256]{3,2,1,0:T(8,128)(2,1)}), bf16[8,2,128,256]{3,2,1,0:T(8,128)(2,1)S(1)}, u32[]{:S(2)}, u32[]{:S(2)}) async-start(bf16[8,2,128,256]{3,2,1,0:T(8,128)(2,1)} %copy-done.7), calls=%async_computation.5 | async-start | bytes 2097152 | tf_op jit(solution)/shard_map/all_to_all | solution.py:161
  164.1 10.2 %collective-permute-done.13.refs_1_ = bf16[6,128,256]{2,1,0:T(8,128)(2,1)S(1)} collective-permute-done((bf16[6,128,256]{2,1,0:T(8,128)(2,1)}, bf16[6,128,256]{2,1,0:T(8,128)(2,1)S(1)}, u32[]{:S(2)}, u32[]{:S(2)}) %collective-permute-start.13) | collective-permute-done | bytes 393248 | tf_op jit(solution)/shard_map/ppermute | solution.py:150
  177.7 4.6 %collective-permute-done.14 = bf16[3,128,256]{2,1,0:T(8,128)(2,1)S(1)} collective-permute-done((bf16[3,128,256]{2,1,0:T(8,128)(2,1)S(1)}, bf16[3,128,256]{2,1,0:T(8,128)(2,1)S(1)}, u32[]{:S(2)}, u32[]{:S(2)}) %collective-permute-start.14) | collective-permute-done | bytes 196640 | tf_op jit(solution)/shard_map/ppermute | solution.py:150
  200.1 13.8 %all-to-all-done.4.refs_1_ = bf16[8,3,128,256]{3,2,1,0:T(8,128)(2,1)S(1)} async-done(((bf16[8,3,128,256]{3,2,1,0:T(8,128)(2,1)}), bf16[8,3,128,256]{3,2,1,0:T(8,128)(2,1)S(1)}, u32[]{:S(2)}, u32[]{:S(2)}) %all-to-all-start.4) | async-done | bytes 1572896 | tf_op jit(solution)/shard_map/all_to_all | solution.py:161
  215.0 5.0 %hop_last.3 = (bf16[768,256]{1,0:T(8,128)(2,1)S(1)}, bf16[768,256]{1,0:T(8,128)(2,1)}) custom-call(bf16[72,768,128]{2,1,0:T(8,128)(2,1)} %densify.1.refs_0_, bf16[8,3,128,256]{3,2,1,0:T(8,128)(2,1)S(1)} %all-to-all-done.4.refs_1_, f32[768,256]{1,0:T(8,128)S(1)} %copy-done.9, f32[768,256]{1,0:T(8,128)S(1)} %mul.28.refs_3_), custom_call_target="tpu_custom_call" | custom-call | tf_op jit(solution)/shard_map/hop_last/pallas_call | solution.py:136
  234.0 6.6 %collective-permute-done.17 = bf16[192,1024]{1,0:T(8,128)(2,1)S(1)} collective-permute-done((bf16[192,1024]{1,0:T(8,128)(2,1)S(1)}, bf16[192,1024]{1,0:T(8,128)(2,1)S(1)}, u32[]{:S(2)}, u32[]{:S(2)}) %collective-permute-start.17) | collective-permute-done | bytes 393248 | tf_op jit(solution)/shard_map/ppermute | solution.py:150
  246.3 7.6 %collective-permute-done.20 = bf16[192,1024]{1,0:T(8,128)(2,1)S(1)} collective-permute-done((bf16[192,1024]{1,0:T(8,128)(2,1)S(1)}, bf16[192,1024]{1,0:T(8,128)(2,1)S(1)}, u32[]{:S(2)}, u32[]{:S(2)}) %collective-permute-start.20) | collective-permute-done | bytes 393248 | tf_op jit(solution)/shard_map/ppermute | solution.py:150
  282.4 8.0 %all-to-all-start.9 = ((f32[32,1,1024]{2,1,0:T(1,128)}), f32[32,1,1024]{2,1,0:T(1,128)S(1)}, u32[]{:S(2)}, u32[]{:S(2)}) async-start(f32[32,1,1024]{2,1,0:T(1,128)} %broadcast_in_dim.4), calls=%async_computation.9 | async-start | bytes 262144 | tf_op jit(solution)/shard_map/all_to_all | solution.py:220
  290.5 6.4 %all-to-all-done.9 = f32[32,1,1024]{2,1,0:T(1,128)S(1)} async-done(((f32[32,1,1024]{2,1,0:T(1,128)}), f32[32,1,1024]{2,1,0:T(1,128)S(1)}, u32[]{:S(2)}, u32[]{:S(2)}) %all-to-all-start.9) | async-done | bytes 131104 | tf_op jit(solution)/shard_map/all_to_all | solution.py:220
  297.6 4.4 %all-to-all-start.10 = ((f32[8,1,1024]{2,1,0:T(1,128)}), f32[8,1,1024]{2,1,0:T(1,128)S(1)}, u32[]{:S(2)}, u32[]{:S(2)}) async-start(f32[8,1,1024]{2,1,0:T(1,128)} %broadcast_in_dim.5), calls=%async_computation.10 | async-start | bytes 65536 | tf_op jit(solution)/shard_map/all_to_all | solution.py:220
  302.8 7.3 %all-to-all-done.10 = f32[8,1,1024]{2,1,0:T(1,128)S(1)} async-done(((f32[8,1,1024]{2,1,0:T(1,128)}), f32[8,1,1024]{2,1,0:T(1,128)S(1)}, u32[]{:S(2)}, u32[]{:S(2)}) %all-to-all-start.10) | async-done | bytes 32800 | tf_op jit(solution)/shard_map/all_to_all | solution.py:220
  314.1 9.1 %all-to-all-done.8 = bf16[8,16,768]{2,1,0:T(8,128)(2,1)S(1)} async-done(((bf16[8,16,768]{2,1,0:T(8,128)(2,1)}), bf16[8,16,768]{2,1,0:T(8,128)(2,1)S(1)}, u32[]{:S(2)}, u32[]{:S(2)}) %all-to-all-start.8) | async-done | bytes 196640 | tf_op jit(solution)/shard_map/all_to_all | solution.py:244
  (185 shorter events, 144.1 us)
Async XLA Ops:
  12.6 24.3 %all-to-all-start.3 = ((bf16[8,1,128,256]{3,2,1,0:T(8,128)(2,1)}), bf16[8,1,128,256]{3,2,1,0:T(8,128)(2,1)S(1)}, u32[]{:S(2)}, u32[]{:S(2)}) async-start(bf16[8,1,128,256]{3,2,1,0:T(8,128)(2,1)} %pick.11), calls=%async_computation.3 | async-start | bytes 1048576 | tf_op jit(solution)/shard_map/all_to_all | solution.py:161
  16.9 14.9 %collective-permute-start = (bf16[6,128,256]{2,1,0:T(8,128)(2,1)S(1)}, bf16[6,128,256]{2,1,0:T(8,128)(2,1)S(1)}, u32[]{:S(2)}, u32[]{:S(2)}) collective-permute-start(bf16[6,128,256]{2,1,0:T(8,128)(2,1)S(1)} %bitcast.83), channel_id=1, source_target_pairs={{0,224},{32,0},{64,32},{96,64},{128,96},{160,128},{192,160},{224,1... | collective-permute-start | bytes 1179656 | tf_op jit(solution)/shard_map/ppermute | solution.py:150
  22.7 12.5 %collective-permute-start.3 = (bf16[6,128,256]{2,1,0:T(8,128)(2,1)S(1)}, bf16[6,128,256]{2,1,0:T(8,128)(2,1)S(1)}, u32[]{:S(2)}, u32[]{:S(2)}) collective-permute-start(bf16[6,128,256]{2,1,0:T(8,128)(2,1)S(1)} %bitcast.84), channel_id=1, source_target_pairs={{0,32},{32,64},{64,96},{96,128},{128,160},{160,192},{192,224},{224... | collective-permute-start | bytes 1179656 | tf_op jit(solution)/shard_map/ppermute | solution.py:150
  36.8 20.3 %all-to-all-start.2 = ((bf16[8,2,128,256]{3,2,1,0:T(8,128)(2,1)}), bf16[8,2,128,256]{3,2,1,0:T(8,128)(2,1)S(1)}, u32[]{:S(2)}, u32[]{:S(2)}) async-start(bf16[8,2,128,256]{3,2,1,0:T(8,128)(2,1)} %pick.10), calls=%async_computation.2 | async-start | bytes 2097152 | tf_op jit(solution)/shard_map/all_to_all | solution.py:161
  41.5 12.5 %collective-permute-start.4 = (bf16[6,128,256]{2,1,0:T(8,128)(2,1)S(1)}, bf16[6,128,256]{2,1,0:T(8,128)(2,1)S(1)}, u32[]{:S(2)}, u32[]{:S(2)}) collective-permute-start(bf16[6,128,256]{2,1,0:T(8,128)(2,1)S(1)} %collective-permute-done.3.refs_1_), channel_id=1, source_target_pairs={{0,32},{32,64},{64,96},{96,128},{128,160},{160,192},{192,224},{224... | collective-permute-start | bytes 1179656 | tf_op jit(solution)/shard_map/ppermute | solution.py:150
  57.2 26.2 %all-to-all-start.1 = ((bf16[8,2,128,256]{3,2,1,0:T(8,128)(2,1)}), bf16[8,2,128,256]{3,2,1,0:T(8,128)(2,1)S(1)}, u32[]{:S(2)}, u32[]{:S(2)}) async-start(bf16[8,2,128,256]{3,2,1,0:T(8,128)(2,1)} %pick.9), calls=%async_computation.1 | async-start | bytes 2097152 | tf_op jit(solution)/shard_map/all_to_all | solution.py:161
  60.8 12.9 %collective-permute-start.5 = (bf16[6,128,256]{2,1,0:T(8,128)(2,1)}, bf16[6,128,256]{2,1,0:T(8,128)(2,1)S(1)}, u32[]{:S(2)}, u32[]{:S(2)}) collective-permute-start(bf16[6,128,256]{2,1,0:T(8,128)(2,1)} %copy-done.17), channel_id=1, source_target_pairs={{0,32},{32,64},{64,96},{96,128},{128,160},{160,192},{192,224},{224... | collective-permute-start | bytes 1179656 | tf_op jit(solution)/shard_map/ppermute | solution.py:150
  61.4 12.5 %collective-permute-start.2 = (bf16[6,128,256]{2,1,0:T(8,128)(2,1)S(1)}, bf16[6,128,256]{2,1,0:T(8,128)(2,1)S(1)}, u32[]{:S(2)}, u32[]{:S(2)}) collective-permute-start(bf16[6,128,256]{2,1,0:T(8,128)(2,1)S(1)} %collective-permute-done.1.refs_0_), channel_id=1, source_target_pairs={{0,224},{32,0},{64,32},{96,64},{128,96},{160,128},{192,160},{224,1... | collective-permute-start | bytes 1179656 | tf_op jit(solution)/shard_map/ppermute | solution.py:150
  84.4 25.6 %all-to-all-start = ((bf16[8,3,128,256]{3,2,1,0:T(8,128)(2,1)}), bf16[8,3,128,256]{3,2,1,0:T(8,128)(2,1)S(1)}, u32[]{:S(2)}, u32[]{:S(2)}) async-start(bf16[8,3,128,256]{3,2,1,0:T(8,128)(2,1)} %copy-done.2), calls=%async_computation | async-start | bytes 3145728 | tf_op jit(solution)/shard_map/all_to_all | solution.py:161
  116.6 18.3 %all-to-all-start.7 = ((bf16[8,1,128,256]{3,2,1,0:T(8,128)(2,1)}), bf16[8,1,128,256]{3,2,1,0:T(8,128)(2,1)S(1)}, u32[]{:S(2)}, u32[]{:S(2)}) async-start(bf16[8,1,128,256]{3,2,1,0:T(8,128)(2,1)} %pick.15), calls=%async_computation.7 | async-start | bytes 1048576 | tf_op jit(solution)/shard_map/all_to_all | solution.py:161
  120.2 13.1 %collective-permute-start.11 = (bf16[6,128,256]{2,1,0:T(8,128)(2,1)}, bf16[6,128,256]{2,1,0:T(8,128)(2,1)S(1)}, u32[]{:S(2)}, u32[]{:S(2)}) collective-permute-start(bf16[6,128,256]{2,1,0:T(8,128)(2,1)} %bitcast.87), channel_id=1, source_target_pairs={{0,32},{32,64},{64,96},{96,128},{128,160},{160,192},{192,224},{224... | collective-permute-start | bytes 1179656 | tf_op jit(solution)/shard_map/ppermute | solution.py:150
  120.3 13.0 %collective-permute-start.8 = (bf16[6,128,256]{2,1,0:T(8,128)(2,1)}, bf16[6,128,256]{2,1,0:T(8,128)(2,1)S(1)}, u32[]{:S(2)}, u32[]{:S(2)}) collective-permute-start(bf16[6,128,256]{2,1,0:T(8,128)(2,1)} %bitcast.88), channel_id=1, source_target_pairs={{0,224},{32,0},{64,32},{96,64},{128,96},{160,128},{192,160},{224,1... | collective-permute-start | bytes 1179656 | tf_op jit(solution)/shard_map/ppermute | solution.py:150
  135.8 20.6 %all-to-all-start.6 = ((bf16[8,2,128,256]{3,2,1,0:T(8,128)(2,1)}), bf16[8,2,128,256]{3,2,1,0:T(8,128)(2,1)S(1)}, u32[]{:S(2)}, u32[]{:S(2)}) async-start(bf16[8,2,128,256]{3,2,1,0:T(8,128)(2,1)} %pick.14), calls=%async_computation.6 | async-start | bytes 2097152 | tf_op jit(solution)/shard_map/all_to_all | solution.py:161
  140.2 80.7 %all-gather.2.cloned.1.call-start = ((), (), s32[]{:S(2)}) async-start(), calls=%async_computation.11 | async-start | bytes 1597440 | tf_op jit(solution)/shard_map/all_gather | solution.py:270
  140.9 13.1 %collective-permute-start.12 = (bf16[6,128,256]{2,1,0:T(8,128)(2,1)S(1)}, bf16[6,128,256]{2,1,0:T(8,128)(2,1)S(1)}, u32[]{:S(2)}, u32[]{:S(2)}) collective-permute-start(bf16[6,128,256]{2,1,0:T(8,128)(2,1)S(1)} %collective-permute-done.11.refs_1_), channel_id=1, source_target_pairs={{0,32},{32,64},{64,96},{96,128},{128,160},{160,192},{192,224},{224... | collective-permute-start | bytes 1179656 | tf_op jit(solution)/shard_map/ppermute | solution.py:150
  141.0 13.0 %collective-permute-start.9 = (bf16[6,128,256]{2,1,0:T(8,128)(2,1)S(1)}, bf16[6,128,256]{2,1,0:T(8,128)(2,1)S(1)}, u32[]{:S(2)}, u32[]{:S(2)}) collective-permute-start(bf16[6,128,256]{2,1,0:T(8,128)(2,1)S(1)} %collective-permute-done.8.refs_0_), channel_id=1, source_target_pairs={{0,224},{32,0},{64,32},{96,64},{128,96},{160,128},{192,160},{224,1... | collective-permute-start | bytes 1179656 | tf_op jit(solution)/shard_map/ppermute | solution.py:150
  156.4 27.8 %all-to-all-start.5 = ((bf16[8,2,128,256]{3,2,1,0:T(8,128)(2,1)}), bf16[8,2,128,256]{3,2,1,0:T(8,128)(2,1)S(1)}, u32[]{:S(2)}, u32[]{:S(2)}) async-start(bf16[8,2,128,256]{3,2,1,0:T(8,128)(2,1)} %copy-done.7), calls=%async_computation.5 | async-start | bytes 2097152 | tf_op jit(solution)/shard_map/all_to_all | solution.py:161
  160.8 13.4 %collective-permute-start.13 = (bf16[6,128,256]{2,1,0:T(8,128)(2,1)}, bf16[6,128,256]{2,1,0:T(8,128)(2,1)S(1)}, u32[]{:S(2)}, u32[]{:S(2)}) collective-permute-start(bf16[6,128,256]{2,1,0:T(8,128)(2,1)} %copy-done.16), channel_id=1, source_target_pairs={{0,32},{32,64},{64,96},{96,128},{128,160},{160,192},{192,224},{224... | collective-permute-start | bytes 1179656 | tf_op jit(solution)/shard_map/ppermute | solution.py:150
  160.8 13.5 %collective-permute-start.10 = (bf16[6,128,256]{2,1,0:T(8,128)(2,1)S(1)}, bf16[6,128,256]{2,1,0:T(8,128)(2,1)S(1)}, u32[]{:S(2)}, u32[]{:S(2)}) collective-permute-start(bf16[6,128,256]{2,1,0:T(8,128)(2,1)S(1)} %collective-permute-done.9.refs_0_), channel_id=1, source_target_pairs={{0,224},{32,0},{64,32},{96,64},{128,96},{160,128},{192,160},{224,1... | collective-permute-start | bytes 1179656 | tf_op jit(solution)/shard_map/ppermute | solution.py:150
  185.2 28.7 %all-to-all-start.4 = ((bf16[8,3,128,256]{3,2,1,0:T(8,128)(2,1)}), bf16[8,3,128,256]{3,2,1,0:T(8,128)(2,1)S(1)}, u32[]{:S(2)}, u32[]{:S(2)}) async-start(bf16[8,3,128,256]{3,2,1,0:T(8,128)(2,1)} %copy-done.1), calls=%async_computation.4 | async-start | bytes 3145728 | tf_op jit(solution)/shard_map/all_to_all | solution.py:161
  278.3 23.7 %collective-permute-start.26 = (bf16[128,768]{1,0:T(8,128)(2,1)S(1)}, bf16[128,768]{1,0:T(8,128)(2,1)S(1)}, u32[]{:S(2)}, u32[]{:S(2)}) collective-permute-start(bf16[128,768]{1,0:T(8,128)(2,1)S(1)} %pad_maximum_fusion.5), channel_id=1, source_target_pairs={{0,8},{8,16},{16,24},{24,0},{1,9},{9,17},{17,25},{25,1},{2,10},{10... | collective-permute-start | bytes 589832 | tf_op jit(solution)/shard_map/ppermute | solution.py:150
  279.0 23.0 %collective-permute-start.28 = (bf16[128,768]{1,0:T(8,128)(2,1)S(1)}, bf16[128,768]{1,0:T(8,128)(2,1)S(1)}, u32[]{:S(2)}, u32[]{:S(2)}) collective-permute-start(bf16[128,768]{1,0:T(8,128)(2,1)S(1)} %pad_maximum_fusion.6), channel_id=1, source_target_pairs={{0,24},{8,0},{16,8},{24,16},{1,25},{9,1},{17,9},{25,17},{2,26},{10... | collective-permute-start | bytes 589832 | tf_op jit(solution)/shard_map/ppermute | solution.py:150
  282.4 14.5 %all-to-all-start.9 = ((f32[32,1,1024]{2,1,0:T(1,128)}), f32[32,1,1024]{2,1,0:T(1,128)S(1)}, u32[]{:S(2)}, u32[]{:S(2)}) async-start(f32[32,1,1024]{2,1,0:T(1,128)} %broadcast_in_dim.4), calls=%async_computation.9 | async-start | bytes 262144 | tf_op jit(solution)/shard_map/all_to_all | solution.py:220
  310.1 13.1 %all-to-all-start.8 = ((bf16[8,16,768]{2,1,0:T(8,128)(2,1)}), bf16[8,16,768]{2,1,0:T(8,128)(2,1)S(1)}, u32[]{:S(2)}, u32[]{:S(2)}) async-start(bf16[8,16,768]{2,1,0:T(8,128)(2,1)} %bitcast.27), calls=%async_computation.8 | async-start | bytes 393216 | tf_op jit(solution)/shard_map/all_to_all | solution.py:244
  (47 other events, 258.0 us)
Sparse Core Ops, SparseCore 0:
  144.3 76.5 all-gather.1
